TPU v7x, 32 devices: a whole 2x2x4 slice. The times are simulated.
32 devices in a mesh: term: 8 (over z, x), sector: 4 (over y, core).
Axes of the slice: x: 2, y: 2, z: 4, core: 2. Of those that a mesh axis runs over, the one named last changes fastest.
Arguments:
- psi_start: float32 [4, 384, 384], P('sector'), may hold values from -6 to 6
- diagonal: float32 [4, 384, 384], P('sector'), may hold values from -3 to 3
- left_ops: float32 [128, 384, 384], P(('term', 'sector')), may hold values from -0.3125 to 0.3125
- right_ops: float32 [128, 384, 384], P(('term', 'sector')), may hold values from -0.078125 to 0.078125
- pair_in: int32 [32, 4], P(('term', 'sector')), may hold values from 0 to 3
- pair_out: int32 [32, 4], P(('term', 'sector')), may hold values from 0 to 3
- pair_count: int32 [32], P(('term', 'sector')), may hold values from 1 to 4, as said below
Outputs:
- psi_final: float32 [4, 384, 384], P('sector')
- energies: float32 [2], replicated
Inputs may be any that keep to these rules, and one draw needn't show every extreme that they name: `pair_count`: some device has all 4 slots live in every draw.
All inputs are finite; a program needn't handle non-finite values.
Results may differ from a plain program's by a relative error of at most 0.00013.
Values sent between devices are 32-bit elements; how exact they have to be, the bound alone decides.
No kernel may reach another device: no remote copies, remote signals or barrier semaphores. Data moves between devices by JAX's collectives and lax.ppermute only.
A program may use at most 64 MiB of HBM per device.

v0:
```python
import jax
import jax.numpy as jnp
from jax import lax
from jax.sharding import PartitionSpec as P

ITERS = 2
epsilon = 1e-06


def apply_pairs(gathered, left_ops, right_ops, pair_in, pair_out, pair_count):

    def one_pair(pair_slot, partial_value):
        source = lax.dynamic_index_in_dim(gathered, pair_in[0, pair_slot], 0, keepdims=False)
        left_block = lax.dynamic_index_in_dim(left_ops, pair_slot, 0, keepdims=False)
        right_block = lax.dynamic_index_in_dim(right_ops, pair_slot, 0, keepdims=False)
        inner_prod = jnp.dot(left_block, source, precision=lax.Precision.HIGHEST)
        product = lax.dot_general(
            inner_prod, right_block, (((1,), (1,)), ((), ())), precision=lax.Precision.HIGHEST
        )
        target = pair_out[0, pair_slot]
        current = lax.dynamic_index_in_dim(partial_value, target, 0, keepdims=False)
        return lax.dynamic_update_index_in_dim(partial_value, current + product, target, 0)

    return lax.fori_loop(0, pair_count[0], one_pair, jnp.zeros(gathered.shape, jnp.float32))


def global_sums(values):
    return lax.psum((values[0],), "sector")


def sigma_blocks(vector, left_ops, right_ops, pair_in, pair_out, pair_count):
    gathered = lax.all_gather(vector, "sector", axis=0, tiled=True)
    partial_value = apply_pairs(gathered, left_ops, right_ops, pair_in, pair_out, pair_count)
    owned_sum = lax.psum_scatter(partial_value, "sector", scatter_dimension=0, tiled=True)
    return lax.psum(owned_sum, "term")


def shards(psi_start, diagonal, left_ops, right_ops, pair_in, pair_out, pair_count):
    vector = psi_start
    cell_total = float(
        psi_start.shape[0] * lax.axis_size("sector") * psi_start.shape[1] * psi_start.shape[2]
    )
    energies = []
    for sweep in range(ITERS):
        vec_share = vector
        squares = global_sums((jnp.sum(vec_share * vec_share),))[0]
        inverse_norm = 1.0 / jnp.sqrt(squares / cell_total + epsilon)
        normed = vector * inverse_norm
        sigma = sigma_blocks(normed, left_ops, right_ops, pair_in, pair_out, pair_count)
        product_sum = global_sums((jnp.sum(normed * sigma),))[0]
        rayleigh = product_sum / cell_total
        residual = sigma - rayleigh * normed
        correction = residual / jnp.maximum(jnp.abs(diagonal - rayleigh), 1.0)
        updated = normed - correction
        vector = updated
        energies.append(rayleigh)
    return (vector, jnp.stack(energies))


def solution(mesh):
    return jax.shard_map(
        shards,
        mesh=mesh,
        in_specs=(
            P("sector", None, None),
            P("sector", None, None),
            P(("term", "sector"), None, None),
            P(("term", "sector"), None, None),
            P(("term", "sector"), None),
            P(("term", "sector"), None),
            P(("term", "sector")),
        ),
        out_specs=(P("sector", None, None), P()),
        check_vma=False,
    )
```

profile of v0, /device:TPU:0, one launch (start us, length us, event | category | flops | bytes accessed | tf_op | source)
XLA Modules:
  0.0 407.2 jit_solution(11676332899711747829)
XLA Ops:
  7.2 1.8 multiply_reduce_fusion.3
  9.1 9.0 %psum.42 = f32[]{:T(128)} all-reduce(f32[]{:T(128)} %multiply_reduce_fusion.3), channel_id=1, replica_groups=mesh['term'=8,'sector'=4] {'sector'}, use_global_device_ids=true, to_apply=%region_1.0 | all-reduce | flops 1 | bytes 8 | tf_op jit(solution)/shard_map/psum | solution.py:28
  18.7 1.9 broadcast_multiply_fusion.1
  20.7 24.4 %all-gather.3.cloned.1.call-done = f32[4,384,384]{2,1,0:T(8,128)} async-done(((f32[1,384,384]{2,1,0:T(8,128)}), f32[4,384,384]{2,1,0:T(8,128)}) %all-gather.3.cloned.1.call-update) | async-done | bytes 2359312 | tf_op jit(solution)/shard_map/all_gather | solution.py:32
  45.4 39.8 %while.20 = (s32[]{:T(128)}, f32[4,384,384]{2,1,0:T(8,128)S(1)}, s32[]{:T(128)}, s32[1,4]{1,0:T(1,128)S(1)}, f32[4,384,384]{2,1,0:T(8,128)}, /*index=5*/s32[1,4]...) while((s32[]{:T(128)}, f32[4,384,384]{2,1,0:T(8,128)S(1)}, ...), condition=%wide.region_3.4_spmd, body=%wide.region_2.3_spmd.sunk | while | flops 1359101952 | bytes 5308675 | solution.py:24
  50.2 2.5 fusion.40
  52.8 2.3 fusion.41
  60.0 2.5 fusion.40
  62.6 2.3 fusion.41
  69.8 2.5 fusion.40
  72.4 2.3 fusion.41
  79.6 2.5 fusion.40
  82.1 2.3 fusion.41
  86.6 32.9 %reduce-scatter.3.cloned.1.call-done = f32[1,384,384]{2,1,0:T(8,128)} async-done(((f32[4,384,384]{2,1,0:T(8,128)}), f32[1,384,384]{2,1,0:T(8,128)}) %reduce-scatter.3.cloned.1.call-update) | async-done | bytes 589840 | tf_op jit(solution)/shard_map/reduce_scatter | solution.py:34
  119.6 76.6 %all-reduce.3.cloned.1.call-done = f32[1,384,384]{2,1,0:T(8,128)} async-done(((f32[1,384,384]{2,1,0:T(8,128)}), f32[1,384,384]{2,1,0:T(8,128)}) %all-reduce.3.cloned.1.call-update) | async-done | bytes 589840 | tf_op jit(solution)/shard_map/psum | solution.py:35
  198.0 6.3 %psum.44 = f32[]{:T(128)} all-reduce(f32[]{:T(128)} %multiply_reduce_fusion.2), channel_id=1, replica_groups=mesh['term'=8,'sector'=4] {'sector'}, use_global_device_ids=true, to_apply=%region_7.8 | all-reduce | flops 1 | bytes 8 | tf_op jit(solution)/shard_map/psum | solution.py:28
  204.9 1.9 multiply_reduce_fusion.1
  206.8 7.2 %psum.45 = f32[]{:T(128)} all-reduce(f32[]{:T(128)} %get-tuple-element.122), channel_id=1, replica_groups=mesh['term'=8,'sector'=4] {'sector'}, use_global_device_ids=true, to_apply=%region_9.10 | all-reduce | flops 1 | bytes 8 | tf_op jit(solution)/shard_map/psum | solution.py:28
  215.7 22.5 %all-gather.5.cloned.1.call-done = f32[4,384,384]{2,1,0:T(8,128)} async-done(((f32[1,384,384]{2,1,0:T(8,128)}), f32[4,384,384]{2,1,0:T(8,128)}) %all-gather.5.cloned.1.call-update) | async-done | bytes 2359312 | tf_op jit(solution)/shard_map/all_gather | solution.py:32
  238.3 39.8 %while.21 = (s32[]{:T(128)}, f32[4,384,384]{2,1,0:T(8,128)S(1)}, s32[]{:T(128)}, s32[1,4]{1,0:T(1,128)S(1)}, f32[4,384,384]{2,1,0:T(8,128)}, /*index=5*/s32[1,4]...) while((s32[]{:T(128)}, f32[4,384,384]{2,1,0:T(8,128)S(1)}, ...), condition=%wide.region_11.12_spmd, body=%wide.region_10.11_spmd.sunk | while | flops 1359101952 | bytes 5308675 | solution.py:24
  243.2 2.5 fusion.46
  245.8 2.3 fusion.47
  253.0 2.5 fusion.46
  255.5 2.3 fusion.47
  262.8 2.5 fusion.46
  265.3 2.3 fusion.47
  272.5 2.5 fusion.46
  275.1 2.3 fusion.47
  279.6 32.9 %reduce-scatter.5.cloned.1.call-done = f32[1,384,384]{2,1,0:T(8,128)} async-done(((f32[4,384,384]{2,1,0:T(8,128)}), f32[1,384,384]{2,1,0:T(8,128)}) %reduce-scatter.5.cloned.1.call-update) | async-done | bytes 589840 | tf_op jit(solution)/shard_map/reduce_scatter | solution.py:34
  312.5 76.5 %all-reduce.5.cloned.1.call-done = f32[1,384,384]{2,1,0:T(8,128)} async-done(((f32[1,384,384]{2,1,0:T(8,128)}), f32[1,384,384]{2,1,0:T(8,128)}) %all-reduce.5.cloned.1.call-update) | async-done | bytes 589840 | tf_op jit(solution)/shard_map/psum | solution.py:35
  390.8 6.3 %psum.47 = f32[]{:T(128)} all-reduce(f32[]{:T(128)} %multiply_reduce_fusion), channel_id=1, replica_groups=mesh['term'=8,'sector'=4] {'sector'}, use_global_device_ids=true, to_apply=%region_15.16 | all-reduce | flops 1 | bytes 8 | tf_op jit(solution)/shard_map/psum | solution.py:28
  398.3 2.1 divide_subtract_fusion
  (46 shorter events, 13.6 us)
Async XLA Ops:
  7.2 38.2 %copy-start.4 = (s32[1,4]{1,0:T(1,128)S(1)}, s32[1,4]{1,0:T(1,128)}, u32[]{:S(2)}) copy-start(s32[1,4]{1,0:T(1,128)} %param.16) | copy-start | bytes 52
  7.2 38.2 %copy-start.5 = (s32[1,4]{1,0:T(1,128)S(1)}, s32[1,4]{1,0:T(1,128)}, u32[]{:S(2)}) copy-start(s32[1,4]{1,0:T(1,128)} %param.15) | copy-start | bytes 52
  7.2 38.0 %all-gather.3.cloned.1.call-start = ((), (), s32[]{:S(2)}) async-start(), calls=%async_computation.2 | async-start | bytes 2949120 | tf_op jit(solution)/shard_map/all_gather | solution.py:32
  20.7 98.9 %reduce-scatter.3.cloned.1.call-start = ((), (), s32[]{:S(2)}) async-start(), calls=%async_computation.3 | async-start | bytes 2949120 | tf_op jit(solution)/shard_map/reduce_scatter | solution.py:34
  85.1 1.4 copy-start.1
  85.1 111.0 %copy-start.2 = (f32[1,384,384]{2,1,0:T(8,128)S(1)}, f32[1,384,384]{2,1,0:T(8,128)}, u32[]{:S(2)}) copy-start(f32[1,384,384]{2,1,0:T(8,128)} %param.11) | copy-start | bytes 1769476
  85.2 119.8 %copy-start.3 = (f32[1,384,384]{2,1,0:T(8,128)S(1)}, f32[1,384,384]{2,1,0:T(8,128)}, u32[]{:S(2)}) copy-start(f32[1,384,384]{2,1,0:T(8,128)} %param.12) | copy-start | bytes 1769476
  86.6 109.6 %all-reduce.3.cloned.1.call-start = ((), (), s32[]{:S(2)}) async-start(), calls=%async_computation.4 | async-start | bytes 1179648 | tf_op jit(solution)/shard_map/psum | solution.py:35
  119.6 118.6 %all-gather.5.cloned.1.call-start = ((), (), s32[]{:S(2)}) async-start(), calls=%async_computation.5 | async-start | bytes 2949120 | tf_op jit(solution)/shard_map/all_gather | solution.py:32
  215.6 96.9 %reduce-scatter.5.cloned.1.call-start = ((), (), s32[]{:S(2)}) async-start(), calls=%async_computation.6 | async-start | bytes 2949120 | tf_op jit(solution)/shard_map/reduce_scatter | solution.py:34
  278.1 1.4 copy-start
  279.5 109.5 %all-reduce.5.cloned.1.call-start = ((), (), s32[]{:S(2)}) async-start(), calls=%async_computation.7 | async-start | bytes 1179648 | tf_op jit(solution)/shard_map/psum | solution.py:35
Sparse Core Ops, SparseCore 0:
  20.8 24.3 all-gather.2
  86.7 32.8 reduce-scatter.2
  122.9 73.2 all-reduce.2
  215.7 22.4 all-gather.4
  279.7 32.8 reduce-scatter.4
  315.7 73.2 all-reduce.4
where the time goes:
time: 409 us; the launch traced here: 407 us
  waiting for transfers between devices  266 us (65%)
  matrix products  38.7 us (9%)
  loops' own time  35.8 us (9%)
  blocking collectives  28.7 us (7%)
  between operations  16.9 us (4%)
  other arithmetic  12.8 us (3%)
  local copies, waits for them, and re-layouts  8.2 us (2%)
    psum x2, waiting for transfers between devices, sigma_blocks(): return lax.psum(owned_sum, 'term')  153 us
    reduce_scatter x2, waiting for transfers between devices, sigma_blocks(): lax.psum_scatter(partial_value, 'sector', scatter_dimension=0, tiled=True)  65.8 us
    all_gather x2, waiting for transfers between devices, sigma_blocks(): gathered = lax.all_gather(vector, 'sector', axis=0, tiled=True)  47 us
    another operation x2, loops' own time, apply_pairs(): lax.fori_loop(0, pair_count[0], one_pair, jnp.zeros(gathered.shape, jnp.f...  35.8 us
    psum x4, blocking collectives, global_sums(): return lax.psum((values[0],), 'sector')  28.7 us
    dot_general x8, matrix products, one_pair(): inner_prod = jnp.dot(left_block, source, precision=lax.Precision.HIGHEST)  20 us
    dot_general x8, matrix products, one_pair(): lax.dot_general(inner_prod, right_block, (((1,), (1,)), ((), ())), precis...  18.6 us
  transfers between devices with their start and end apart: 6, of which 6 were waited for; matrix products, arithmetic and copies ran while one was open for 0% of the time, Pallas kernels for 0%

commit v1 on v0

--- a/solution.py
+++ b/solution.py
@@ -5,6 +5,18 @@
 
 ITERS = 2
 epsilon = 1e-06
+
+
+def collect(array, axis, dim):
+    ways, here = (lax.axis_size(axis), lax.axis_index(axis))
+    grown, reach = (array, 1)
+    while reach < ways:
+        theirs = lax.ppermute(grown, axis, [(d, d ^ reach) for d in range(ways)])
+        mine_first = jnp.concatenate([grown, theirs], axis=dim)
+        theirs_first = jnp.concatenate([theirs, grown], axis=dim)
+        grown = jnp.where(here & reach == 0, mine_first, theirs_first)
+        reach = 2 * reach
+    return grown
 
 
 def apply_pairs(gathered, left_ops, right_ops, pair_in, pair_out, pair_count):
@@ -29,7 +41,7 @@
 
 
 def sigma_blocks(vector, left_ops, right_ops, pair_in, pair_out, pair_count):
-    gathered = lax.all_gather(vector, "sector", axis=0, tiled=True)
+    gathered = collect(vector, "sector", 0)
     partial_value = apply_pairs(gathered, left_ops, right_ops, pair_in, pair_out, pair_count)
     owned_sum = lax.psum_scatter(partial_value, "sector", scatter_dimension=0, tiled=True)
     return lax.psum(owned_sum, "term")

time: 409 us -> 422 us (1.032)
  waiting for transfers between devices: 266 us -> 276 us
    ppermute x0 -> x4, waiting for transfers between devices: none -> 58.7 us  [collect(): theirs = lax.ppermute(grown, axis, [(d, d ^ reach) for d in range(ways)])]
    all_gather x2 -> x0, waiting for transfers between devices: 47 us -> none  [sigma_blocks(): gathered = lax.all_gather(vector, 'sector', axis=0, tiled=True)]
  transfers between devices with their start and end apart: 6 -> 8, of which waited for: 6 -> 8; matrix products, arithmetic and copies ran while one was open for 0% -> 0% of each run, Pallas kernels for 0% -> 0%
where the time goes in v1:
time: 422 us; the launch traced here: 421 us
  waiting for transfers between devices  276 us (65%)
  matrix products  38.7 us (9%)
  loops' own time  35.5 us (8%)
  blocking collectives  28.7 us (7%)
  between operations  16.6 us (4%)
  other arithmetic  14.6 us (3%)
  local copies, waits for them, and re-layouts  8.76 us (2%)
    psum x2, waiting for transfers between devices, sigma_blocks(): return lax.psum(owned_sum, 'term')  153 us
    reduce_scatter x2, waiting for transfers between devices, sigma_blocks(): lax.psum_scatter(partial_value, 'sector', scatter_dimension=0, tiled=True)  64.3 us
    ppermute x4, waiting for transfers between devices, collect(): theirs = lax.ppermute(grown, axis, [(d, d ^ reach) for d in range(ways)])  58.7 us
    another operation x2, loops' own time, apply_pairs(): lax.fori_loop(0, pair_count[0], one_pair, jnp.zeros(gathered.shape, jnp.f...  35.5 us
    psum x4, blocking collectives, global_sums(): return lax.psum((values[0],), 'sector')  28.7 us
    dot_general x8, matrix products, one_pair(): inner_prod = jnp.dot(left_block, source, precision=lax.Precision.HIGHEST)  20 us
    dot_general x8, matrix products, one_pair(): lax.dot_general(inner_prod, right_block, (((1,), (1,)), ((), ())), precis...  18.6 us
  transfers between devices with their start and end apart: 8, of which 8 were waited for; matrix products, arithmetic and copies ran while one was open for 0% of the time, Pallas kernels for 0%

profile of v1, /device:TPU:0, one launch (start us, length us, event | category | flops | bytes accessed | tf_op | source)
XLA Modules:
  0.0 420.7 jit_solution(7416440675835193257)
XLA Ops:
  9.0 9.0 %psum.42 = f32[]{:T(128)} all-reduce(f32[]{:T(128)} %multiply_reduce_fusion.3), channel_id=1, replica_groups=mesh['term'=8,'sector'=4] {'sector'}, use_global_device_ids=true, to_apply=%region_1.0 | all-reduce | flops 1 | bytes 8 | tf_op jit(solution)/shard_map/psum | solution.py:40
  19.9 2.0 collective-permute-done
  22.4 27.6 %collective-permute-done.1 = f32[2,384,384]{2,1,0:T(8,128)S(1)} collective-permute-done((f32[2,384,384]{2,1,0:T(8,128)S(1)}, f32[2,384,384]{2,1,0:T(8,128)S(1)}, u32[]{:S(2)}, u32[]{:S(2)}) %collective-permute-start.1) | collective-permute-done | bytes 1179680 | tf_op jit(solution)/shard_map/ppermute | solution.py:14
  52.3 39.8 %while.20 = (s32[]{:T(128)}, f32[4,384,384]{2,1,0:T(8,128)S(1)}, s32[]{:T(128)}, s32[1,4]{1,0:T(1,128)S(1)}, f32[4,384,384]{2,1,0:T(8,128)}, /*index=5*/s32[1,4]...) while((s32[]{:T(128)}, f32[4,384,384]{2,1,0:T(8,128)S(1)}, ...), condition=%wide.region_3.4_spmd, body=%wide.region_2.3_spmd.sunk | while | flops 1359101952 | bytes 5308675 | solution.py:36
  57.2 2.5 fusion.40
  59.7 2.3 fusion.41
  67.0 2.5 fusion.40
  69.5 2.3 fusion.41
  76.7 2.5 fusion.40
  79.3 2.3 fusion.41
  86.5 2.5 fusion.40
  89.1 2.3 fusion.41
  93.5 33.2 %reduce-scatter.3.cloned.1.call-done = f32[1,384,384]{2,1,0:T(8,128)} async-done(((f32[4,384,384]{2,1,0:T(8,128)}), f32[1,384,384]{2,1,0:T(8,128)}) %reduce-scatter.3.cloned.1.call-update) | async-done | bytes 589840 | tf_op jit(solution)/shard_map/reduce_scatter | solution.py:46
  126.8 76.6 %all-reduce.3.cloned.1.call-done = f32[1,384,384]{2,1,0:T(8,128)} async-done(((f32[1,384,384]{2,1,0:T(8,128)}), f32[1,384,384]{2,1,0:T(8,128)}) %all-reduce.3.cloned.1.call-update) | async-done | bytes 589840 | tf_op jit(solution)/shard_map/psum | solution.py:47
  205.2 6.3 %psum.44 = f32[]{:T(128)} all-reduce(f32[]{:T(128)} %multiply_reduce_fusion.2), channel_id=1, replica_groups=mesh['term'=8,'sector'=4] {'sector'}, use_global_device_ids=true, to_apply=%region_7.8 | all-reduce | flops 1 | bytes 8 | tf_op jit(solution)/shard_map/psum | solution.py:40
  212.1 2.1 multiply_reduce_fusion.1
  214.2 7.2 %psum.45 = f32[]{:T(128)} all-reduce(f32[]{:T(128)} %get-tuple-element.122), channel_id=1, replica_groups=mesh['term'=8,'sector'=4] {'sector'}, use_global_device_ids=true, to_apply=%region_9.10 | all-reduce | flops 1 | bytes 8 | tf_op jit(solution)/shard_map/psum | solution.py:40
  222.2 2.0 collective-permute-done.2
  225.3 27.1 %collective-permute-done.3 = f32[2,384,384]{2,1,0:T(8,128)S(1)} collective-permute-done((f32[2,384,384]{2,1,0:T(8,128)S(1)}, f32[2,384,384]{2,1,0:T(8,128)S(1)}, u32[]{:S(2)}, u32[]{:S(2)}) %collective-permute-start.3) | collective-permute-done | bytes 1179680 | tf_op jit(solution)/shard_map/ppermute | solution.py:14
  254.1 39.5 %while.21 = (s32[]{:T(128)}, f32[4,384,384]{2,1,0:T(8,128)S(1)}, s32[]{:T(128)}, s32[1,4]{1,0:T(1,128)S(1)}, f32[4,384,384]{2,1,0:T(8,128)}, /*index=5*/s32[1,4]...) while((s32[]{:T(128)}, f32[4,384,384]{2,1,0:T(8,128)S(1)}, ...), condition=%wide.region_11.12_spmd, body=%wide.region_10.11_spmd.sunk | while | flops 1359101952 | bytes 5308675 | solution.py:36
  258.9 2.5 fusion.46
  261.5 2.3 fusion.47
  268.7 2.5 fusion.46
  271.2 2.3 fusion.47
  278.4 2.5 fusion.46
  280.9 2.3 fusion.47
  288.1 2.5 fusion.46
  290.7 2.3 fusion.47
  295.1 31.1 %reduce-scatter.5.cloned.1.call-done = f32[1,384,384]{2,1,0:T(8,128)} async-done(((f32[4,384,384]{2,1,0:T(8,128)}), f32[1,384,384]{2,1,0:T(8,128)}) %reduce-scatter.5.cloned.1.call-update) | async-done | bytes 589840 | tf_op jit(solution)/shard_map/reduce_scatter | solution.py:46
  326.3 76.5 %all-reduce.5.cloned.1.call-done = f32[1,384,384]{2,1,0:T(8,128)} async-done(((f32[1,384,384]{2,1,0:T(8,128)}), f32[1,384,384]{2,1,0:T(8,128)}) %all-reduce.5.cloned.1.call-update) | async-done | bytes 589840 | tf_op jit(solution)/shard_map/psum | solution.py:47
  404.6 6.3 %psum.47 = f32[]{:T(128)} all-reduce(f32[]{:T(128)} %multiply_reduce_fusion), channel_id=1, replica_groups=mesh['term'=8,'sector'=4] {'sector'}, use_global_device_ids=true, to_apply=%region_15.16 | all-reduce | flops 1 | bytes 8 | tf_op jit(solution)/shard_map/psum | solution.py:40
  412.1 2.1 divide_subtract_fusion
  (52 shorter events, 21.0 us)
Async XLA Ops:
  7.2 119.6 %reduce-scatter.3.cloned.1.call-start = ((), (), s32[]{:S(2)}) async-start(), calls=%async_computation.2 | async-start | bytes 2949120 | tf_op jit(solution)/shard_map/reduce_scatter | solution.py:46
  19.8 2.1 collective-permute-start
  22.0 28.1 %collective-permute-start.1 = (f32[2,384,384]{2,1,0:T(8,128)S(1)}, f32[2,384,384]{2,1,0:T(8,128)S(1)}, u32[]{:S(2)}, u32[]{:S(2)}) collective-permute-start(f32[2,384,384]{2,1,0:T(8,128)S(1)} %maximum_select_fusion.2), channel_id=1, source_target_pairs={{0,2},{1,3},{2,0},{3,1},{4,6},{5,7},{6,4},{7,5},{8,10},{9,11},{10,... | collective-permute-start | bytes 3538952 | tf_op jit(solution)/shard_map/ppermute | solution.py:14
  51.6 0.7 copy-start.4
  51.6 0.7 copy-start.5
  92.1 1.4 copy-start.1
  92.1 111.3 %copy-start.2 = (f32[1,384,384]{2,1,0:T(8,128)S(1)}, f32[1,384,384]{2,1,0:T(8,128)}, u32[]{:S(2)}) copy-start(f32[1,384,384]{2,1,0:T(8,128)} %param.11) | copy-start | bytes 1769476
  93.5 109.9 %all-reduce.3.cloned.1.call-start = ((), (), s32[]{:S(2)}) async-start(), calls=%async_computation.3 | async-start | bytes 1179648 | tf_op jit(solution)/shard_map/psum | solution.py:47
  126.8 199.5 %reduce-scatter.5.cloned.1.call-start = ((), (), s32[]{:S(2)}) async-start(), calls=%async_computation.4 | async-start | bytes 2949120 | tf_op jit(solution)/shard_map/reduce_scatter | solution.py:46
  222.2 2.1 collective-permute-start.2
  224.3 28.1 %collective-permute-start.3 = (f32[2,384,384]{2,1,0:T(8,128)S(1)}, f32[2,384,384]{2,1,0:T(8,128)S(1)}, u32[]{:S(2)}, u32[]{:S(2)}) collective-permute-start(f32[2,384,384]{2,1,0:T(8,128)S(1)} %maximum_select_fusion.3), channel_id=1, source_target_pairs={{0,2},{1,3},{2,0},{3,1},{4,6},{5,7},{6,4},{7,5},{8,10},{9,11},{10,... | collective-permute-start | bytes 3538952 | tf_op jit(solution)/shard_map/ppermute | solution.py:14
  293.7 1.4 copy-start
  293.7 118.5 %copy-start.3 = (f32[1,384,384]{2,1,0:T(8,128)S(1)}, f32[1,384,384]{2,1,0:T(8,128)}, u32[]{:S(2)}) copy-start(f32[1,384,384]{2,1,0:T(8,128)} %param.12) | copy-start | bytes 1769476
  295.1 107.7 %all-reduce.5.cloned.1.call-start = ((), (), s32[]{:S(2)}) async-start(), calls=%async_computation.5 | async-start | bytes 1179648 | tf_op jit(solution)/shard_map/psum | solution.py:47
Sparse Core Ops, SparseCore 0:
  93.6 33.0 reduce-scatter.2
  130.1 73.2 all-reduce.2
  295.2 31.0 reduce-scatter.4
  329.5 73.2 all-reduce.4
